TPU v7x, 32 devices: a whole 2x2x4 slice. The times are simulated.
32 devices in a mesh: grp: 8 (over y, x, core), tp: 4 (over z).
Axes of the slice: x: 2, y: 2, z: 4, core: 2. Of those that a mesh axis runs over, the one named last changes fastest.
Arguments:
- text_embeds: bfloat16 [16384, 8192], P('grp', 'tp'), may hold values from -6 to 6
- image_embeds: bfloat16 [8192, 8192], P(('grp', 'tp')), may hold values from -6 to 6
- image_offsets: int32 [16, 2], P('grp'), may hold values from 0 to 768, as said below
- image_counts: int32 [16], P('grp'), may hold values from 1 to 2
- seq_lengths: int32 [16], P('grp'), may hold values from 513 to 1024
- norm_gain: bfloat16 [8192], P('tp'), may hold values from 0.25 to 1.75
- key_weight: bfloat16 [8192, 512], P('tp'), may hold values from -0.0625 to 0.0625
- key_bias: bfloat16 [512], replicated, may hold values from -3 to 3
- key_cotangent: bfloat16 [16384, 512], P(('grp', 'tp')), may hold values from -0.017944336 to 0.017944336
Outputs:
- key_states: bfloat16 [16384, 512], P(('grp', 'tp'))
- weight_grad: float32 [8192, 512], P('tp')
- bias_grad: float32 [512], replicated
- gain_grad: float32 [8192], P('tp')
Inputs may be any that keep to these rules, and one draw needn't show every extreme that they name: `image_offsets`: each sequence's first image_counts slots hold increasing starts of non-intersecting runs of 256 rows that end within its used rows; later slots hold 0.
All inputs are finite; a program needn't handle non-finite values.
Results may differ from a plain program's by a relative error of at most 0.0046.
Values may be sent and summed in bfloat16 or wider, within the bound.
A program may use at most 64 MiB of HBM per device.

v0:
```python
import jax
import jax.numpy as jnp
from jax import lax
from jax.sharding import PartitionSpec as P

EPS = 1e-06
F32 = jnp.float32
BF16 = jnp.bfloat16


def on_device(
    text_embeds,
    image_embeds,
    image_offsets,
    image_counts,
    seq_lengths,
    norm_gain,
    key_weight,
    key_bias,
    key_cotangent,
):
    n_tp = lax.axis_size("tp")
    me = lax.axis_index("tp")
    rows = text_embeds.shape[0]
    width = image_embeds.shape[1]
    seqs, slots = image_offsets.shape
    length = rows // seqs
    own_image = image_embeds.shape[0]
    image_total = own_image * n_tp
    patch = image_total // (seqs * slots)
    own_count = key_cotangent.shape[0]
    image_rows = lax.all_to_all(image_embeds, "tp", split_axis=1, concat_axis=0, tiled=True)
    position = lax.broadcasted_iota(jnp.int32, (seqs, length), 1)
    row_valid = (position < seq_lengths[:, None]).astype(F32).reshape(rows)
    own_valid = lax.dynamic_slice_in_dim(row_valid, me * own_count, own_count, 0)
    own_grad = lax.optimization_barrier(
        (key_cotangent.astype(F32) * own_valid[:, None]).astype(BF16)
    )
    masked_grad = lax.all_gather(own_grad, "tp", axis=0, tiled=True)
    bias_grad = lax.psum(jnp.sum(own_grad.astype(F32), axis=0), ("grp", "tp"))
    text32 = text_embeds.astype(F32)
    image32 = image_embeds.astype(F32)
    image_squares = lax.dynamic_update_slice_in_dim(
        jnp.zeros((image_total,), F32), jnp.sum(image32 * image32, axis=1), me * own_image, 0
    )
    squares = lax.psum(jnp.concatenate([jnp.sum(text32 * text32, axis=1), image_squares]), "tp")
    rstd = lax.rsqrt(squares / width + EPS)
    slot_used = lax.broadcasted_iota(jnp.int32, (seqs, slots), 1) < image_counts[:, None]
    inside = jnp.zeros((seqs, length), jnp.bool_)
    source = jnp.zeros((seqs, length), jnp.int32)
    first = lax.broadcasted_iota(jnp.int32, (seqs, length), 0) * (slots * patch)
    for k in range(slots):
        start = image_offsets[:, k : k + 1]
        here = slot_used[:, k : k + 1] & (position >= start) & (position < start + patch)
        source = jnp.where(here, first + k * patch + position - start, source)
        inside = inside | here
    text_rstd = rstd[:rows] * (1.0 - inside.astype(F32).reshape(rows))
    image_rstd = rstd[rows:]
    used = jnp.repeat(slot_used.reshape(-1).astype(F32), patch)
    gain32 = norm_gain.astype(F32)
    scaled_weight = (key_weight.astype(F32) * gain32[:, None]).astype(BF16)
    partial = (
        jnp.dot(text_embeds, scaled_weight, preferred_element_type=F32) * text_rstd[:, None]
    ).astype(BF16)
    text_grad = (masked_grad.astype(F32) * text_rstd[:, None]).astype(BF16)
    slot_starts = (
        lax.broadcasted_iota(jnp.int32, (seqs, slots), 0) * length + image_offsets
    ).reshape(-1)
    image_at = (
        slot_starts[:, None] + lax.broadcasted_iota(jnp.int32, (seqs * slots, patch), 1)
    ).reshape(-1)
    picked = jnp.take(masked_grad, image_at, axis=0, mode="clip")
    image_grad = (picked.astype(F32) * (image_rstd * used)[:, None]).astype(BF16)
    over_rows = (((0,), (0,)), ((), ()))
    text_part = lax.dot_general(text_embeds, text_grad, over_rows, preferred_element_type=F32)
    image_keys = (
        jnp.dot(image_rows, scaled_weight, preferred_element_type=F32) * image_rstd[:, None]
    ).astype(BF16)
    placed = jnp.take(image_keys, source.reshape(rows), axis=0, mode="clip")
    partial = jnp.where(inside.reshape(rows)[:, None], placed, partial)
    partial, masked_grad, bias_grad = lax.optimization_barrier((partial, masked_grad, bias_grad))
    projected = lax.psum_scatter(partial, "tp", scatter_dimension=0, tiled=True)
    key_states = (
        (projected.astype(F32) + key_bias.astype(F32)[None, :]) * own_valid[:, None]
    ).astype(BF16)
    image_part = lax.dot_general(image_rows, image_grad, over_rows, preferred_element_type=F32)
    total = lax.psum((text_part + image_part).astype(BF16), "grp").astype(F32)
    weight_grad = total * gain32[:, None]
    gain_grad = jnp.sum(total * key_weight.astype(F32), axis=1)
    return (key_states, weight_grad, bias_grad, gain_grad)


def solution(mesh):
    placed = (
        P("grp", "tp"),
        P(("grp", "tp"), None),
        P("grp", None),
        P("grp"),
        P("grp"),
        P("tp"),
        P("tp", None),
        P(),
        P(("grp", "tp"), None),
    )
    return jax.shard_map(
        on_device,
        mesh=mesh,
        in_specs=placed,
        out_specs=(P(("grp", "tp"), None), P("tp", None), P(), P("tp")),
        check_vma=False,
    )
```

profile of v0, /device:TPU:0, one launch (start us, length us, event | category | flops | bytes accessed | tf_op | source)
XLA Modules:
  0.0 348.3 jit_solution(14095932493099703073)
XLA Ops:
  7.2 6.4 %copy.28 = bf16[256,8192]{0,1:T(8,128)(2,1)} copy(bf16[256,8192]{1,0:T(8,128)(2,1)} %param.10) | data formatting | bytes 8388608 | tf_op args[1]
  13.6 6.6 %all-to-all-start = ((bf16[256,4,2048]{0,2,1:T(8,128)(2,1)}), bf16[256,4,2048]{0,2,1:T(8,128)(2,1)}, u32[]{:S(2)}, u32[]{:S(2)}) async-start(bf16[256,4,2048]{0,2,1:T(8,128)(2,1)} %bitcast.74), calls=%async_computation | async-start | bytes 8388608 | tf_op jit(solution)/shard_map/all_to_all | solution.py:32
  20.3 0.2 copy.32
  20.6 0.9 multiply_convert_fusion.7
  21.6 0.2 slice_reduce_fusion.1
  21.8 0.2 add_reduce_fusion.1
  22.0 0.1 and_or_fusion
  22.6 0.1 reshape.320
  22.9 2.5 copy.27
  25.6 3.1 multiply_reduce_fusion.1
  28.7 0.3 dynamic_update_slice.3
  28.9 0.1 convert_reduce_fusion
  29.1 138.5 %psum.22 = f32[512]{0:T(512)} all-reduce(f32[512]{0:T(512)S(1)} %convert_reduce_fusion), channel_id=1, replica_groups=mesh['grp'=8,'tp'=4] {'grp','tp'}, use_global_device_ids=true, to_apply=%region_4.0 | all-reduce | flops 512 | bytes 4096 | tf_op jit(solution)/shard_map/psum | solution.py:40
  167.6 5.1 %multiply_reduce_fusion = f32[2048]{0:T(1024)S(1)} fusion(bf16[2048,2048]{1,0:T(8,128)(2,1)} %param.9), kind=kLoop, calls=%fused_computation.2 | loop fusion | flops 12580864 | bytes 8396800 | tf_op jit(solution)/shard_map/reduce_sum | solution.py:46
  172.7 17.7 %psum.21 = f32[3072]{0:T(1024)S(1)} all-reduce(f32[3072]{0:T(1024)S(1)} %pad_maximum_fusion), channel_id=1, replica_groups=mesh['grp'=8,'tp'=4] {'tp'}, use_global_device_ids=true, to_apply=%region_2.0 | all-reduce | flops 3072 | bytes 24576 | tf_op jit(solution)/shard_map/psum | solution.py:46
  190.5 2.9 copy.33
  193.4 5.1 %gather_fusion.1 = bf16[1024,512]{1,0:T(8,128)(2,1)} fusion(bf16[2048,512]{1,0:T(8,128)(2,1)S(1)} %copy.33, s32[1024]{0:T(1024)S(1)} %broadcast_clamp_fusion.1), kind=kCustom, calls=%fused_computation.1 | custom fusion | bytes 2101248 | tf_op jit(solution)/shard_map/jit(_take)/gather | solution.py:72
  198.5 6.3 %copy.29 = bf16[4,256,2048]{2,1,0:T(8,128)(2,1)} copy(bf16[4,256,2048]{1,2,0:T(8,128)(2,1)} %bitcast.1) | data formatting | bytes 8388608 | tf_op jit(solution)/shard_map/all_to_all | solution.py:32
  204.8 4.6 %fusion.11 = bf16[1024,512]{0,1:T(8,128)(2,1)S(1)} fusion(bf16[1024,2048]{1,0:T(8,128)(2,1)} %bitcast.72, bf16[2048,512]{0,1:T(8,128)(2,1)S(1)} %copy-done, f32[2048]{0:T(1024)S(1)} %convert_element_type.85, f32[1024]{0:T(1024)S(1)} %get-tuple-element.29), kind=kOutput, calls=%fused_computation.19 | convolution fusion | flops 2151677952 | bytes 7352320 | tf_op jit(solution)/shard_map/dot_general | solution.py:77
  209.4 0.5 copy.30
  209.9 7.5 %gather_fusion = bf16[2048,512]{1,0:T(8,128)(2,1)S(1)} fusion(bf16[1024,512]{1,0:T(8,128)(2,1)S(1)} %copy.30, s32[2048]{0:T(1024)S(1)} %broadcast_clamp_fusion), kind=kCustom, calls=%fused_computation | custom fusion | bytes 4202496 | tf_op jit(solution)/shard_map/jit(_take)/gather | solution.py:79
  217.5 2.5 copy.31
  220.0 4.9 %fusion.14 = f32[512,2048]{1,0:T(8,128)S(1)} fusion(bf16[1024,2048]{1,0:T(8,128)(2,1)} %bitcast.73, bf16[1024,512]{1,0:T(8,128)(2,1)S(1)} %copy-done.2, f32[1024]{0:T(1024)S(1)} %get-tuple-element.28), kind=kOutput, calls=%fused_computation.20 | convolution fusion | flops 2149056512 | bytes 9441280 | tf_op jit(solution)/shard_map/dot_general | solution.py:86
  224.9 9.3 %fusion.3 = bf16[2048,512]{0,1:T(8,128)(2,1)} fusion(f32[512,2048]{1,0:T(8,128)S(1)} %fusion.14, bf16[2048,2048]{1,0:T(8,128)(2,1)} %param.9, bf16[2048,512]{0,1:T(8,128)(2,1)S(1)} %copy-done.5, f32[2048]{0:T(1024)S(1)} %slice_multiply_fusion), kind=kOutput, calls=%fused_computation.13 | convolution fusion | flops 4300210176 | bytes 16785408 | tf_op jit(solution)/shard_map/dot_general | solution.py:75
  234.3 0.3 reduce-scatter.2.cloned.1.call-start
  234.5 9.6 %fusion.4 = bf16[2048,512]{0,1:T(8,128)(2,1)} fusion(bf16[2048,512]{0,1:T(8,128)(2,1)} %copy.31, bf16[2048,2048]{1,0:T(8,128)(2,1)} %param.9, f32[2048]{0:T(1024)S(1)} %slice_multiply_fusion, pred[2048]{0:T(1024)(128)(4,1)S(1)} %or.12, bf16[2048,512]{0,1:T(8,128)(2,1)S(1)} %copy-done.1, f32[2048]{0:T(1024)S(1)} %convert_element_type.85), kind=kOutput, calls=%fused_computation.14 | convolution fusion | flops 4301258752 | bytes 14698496 | tf_op jit(solution)/shard_map/dot_general | solution.py:63
  244.2 50.3 %all-reduce.2.cloned.1.call-done = bf16[2048,512]{0,1:T(8,128)(2,1)} async-done(((bf16[2048,512]{0,1:T(8,128)(2,1)}), bf16[2048,512]{0,1:T(8,128)(2,1)}) %all-reduce.2.cloned.1.call-update) | async-done | bytes 2097168 | tf_op jit(solution)/shard_map/psum | solution.py:87
  294.4 4.9 %fusion.1 = (f32[2048]{0:T(1024)}, f32[2048,512]{0,1:T(8,128)}) fusion(bf16[2048,512]{0,1:T(8,128)(2,1)S(1)} %copy-done.1, bf16[2048,512]{0,1:T(8,128)(2,1)} %all-reduce.2.cloned.1.call-done, f32[2048]{0:T(1024)S(1)} %convert_element_type.85), kind=kLoop, calls=%fused_computation.8 | loop fusion | flops 5240832 | bytes 8404992 | tf_op jit(solution)/shard_map/reduce_sum | solution.py:89
  299.4 5.4 %copy.35 = f32[2048,512]{1,0:T(8,128)} copy(f32[2048,512]{0,1:T(8,128)} %get-tuple-element.27) | data formatting | bytes 8388608
  304.8 34.7 %reduce-scatter.2.cloned.1.call-done = bf16[512,512]{0,1:T(8,128)(2,1)} async-done(((bf16[2048,512]{0,1:T(8,128)(2,1)}), bf16[512,512]{0,1:T(8,128)(2,1)}) %reduce-scatter.2.cloned.1.call-update) | async-done | bytes 524304 | tf_op jit(solution)/shard_map/reduce_scatter | solution.py:82
  339.5 1.2 multiply_convert_fusion.6
  340.7 1.0 copy.34
  (69 shorter events, 1.2 us)
Async XLA Ops:
  13.5 6.7 %copy-start.10 = (s32[2]{0:T(128)S(1)}, s32[2]{0:T(128)}, u32[]{:S(2)}) copy-start(s32[2]{0:T(128)} %param.13) | copy-start | bytes 28
  13.5 6.7 %copy-start.6 = (bf16[512,512]{1,0:T(8,128)(2,1)S(1)}, bf16[512,512]{1,0:T(8,128)(2,1)}, u32[]{:S(2)}) copy-start(bf16[512,512]{1,0:T(8,128)(2,1)} %param.17) | copy-start | bytes 1572868
  13.5 8.0 %copy-start.11 = (s32[2]{0:T(128)S(1)}, s32[2]{0:T(128)}, u32[]{:S(2)}) copy-start(s32[2]{0:T(128)} %param.12) | copy-start | bytes 28
  13.5 8.3 %copy-start.7 = (s32[2,2]{1,0:T(2,128)S(1)}, s32[2,2]{1,0:T(2,128)}, u32[]{:S(2)}) copy-start(s32[2,2]{1,0:T(2,128)} %param.11) | copy-start | bytes 52
  13.5 9.3 %copy-start.4 = (bf16[2048,512]{1,0:T(8,128)(2,1)S(1)}, bf16[2048,512]{1,0:T(8,128)(2,1)}, u32[]{:S(2)}) copy-start(bf16[2048,512]{1,0:T(8,128)(2,1)} %param.15) | copy-start | bytes 6291460
  13.6 184.9 %all-to-all-start = ((bf16[256,4,2048]{0,2,1:T(8,128)(2,1)}), bf16[256,4,2048]{0,2,1:T(8,128)(2,1)}, u32[]{:S(2)}, u32[]{:S(2)}) async-start(bf16[256,4,2048]{0,2,1:T(8,128)(2,1)} %bitcast.74), calls=%async_computation | async-start | bytes 8388608 | tf_op jit(solution)/shard_map/all_to_all | solution.py:32
  20.2 5.2 %copy-start.8 = (bf16[2048]{0:T(1024)(128)(2,1)S(1)}, bf16[2048]{0:T(1024)(128)(2,1)}, u32[]{:S(2)}) copy-start(bf16[2048]{0:T(1024)(128)(2,1)} %param.14) | copy-start | bytes 12292
  20.2 170.3 %all-gather.2.cloned.1.call-start = ((), (), s32[]{:S(2)}) async-start(), calls=%async_computation.2 | async-start | bytes 2621440 | tf_op jit(solution)/shard_map/all_gather | solution.py:39
  21.5 273.0 %all-reduce.2.cloned.1.call-start = ((), (), s32[]{:S(2)}) async-start(), calls=%async_computation.4 | async-start | bytes 4194304 | tf_op jit(solution)/shard_map/psum | solution.py:87
  22.8 6.1 %copy-start.3 = (bf16[512,512]{0,1:T(8,128)(2,1)S(1)}, bf16[512,512]{0,1:T(8,128)(2,1)}, u32[]{:S(2)}) copy-start(bf16[512,512]{0,1:T(8,128)(2,1)} %multiply_convert_fusion.7) | copy-start | bytes 1572868
  198.4 6.4 %copy-start = (bf16[2048,512]{0,1:T(8,128)(2,1)S(1)}, bf16[2048,512]{0,1:T(8,128)(2,1)}, u32[]{:S(2)}) copy-start(bf16[2048,512]{0,1:T(8,128)(2,1)} %copy.27) | copy-start | bytes 6291460
  217.5 2.5 copy-start.2
  220.0 4.9 %copy-start.5 = (bf16[2048,512]{0,1:T(8,128)(2,1)S(1)}, bf16[2048,512]{0,1:T(8,128)(2,1)}, u32[]{:S(2)}) copy-start(bf16[2048,512]{0,1:T(8,128)(2,1)} %all-gather.2.cloned.1.call-done) | copy-start | bytes 6291460
  224.9 9.6 %copy-start.1 = (bf16[2048,512]{0,1:T(8,128)(2,1)S(1)}, bf16[2048,512]{0,1:T(8,128)(2,1)}, u32[]{:S(2)}) copy-start(bf16[2048,512]{0,1:T(8,128)(2,1)} %copy.27) | copy-start | bytes 6291460
  234.3 9.9 %copy-start.9 = (bf16[512]{0:T(512)(128)(2,1)S(1)}, bf16[512]{0:T(512)(128)(2,1)}, u32[]{:S(2)}) copy-start(bf16[512]{0:T(512)(128)(2,1)} %param.16) | copy-start | bytes 3076
  234.3 105.2 %reduce-scatter.2.cloned.1.call-start = ((), (), s32[]{:S(2)}) async-start(), calls=%async_computation.3 | async-start | bytes 2621440 | tf_op jit(solution)/shard_map/reduce_scatter | solution.py:82
Sparse Core Ops, SparseCore 0:
  23.1 77.2 all-gather.1
  234.4 60.0 all-reduce.1
  296.7 42.6 reduce-scatter.1
where the time goes:
time: 349 us; the launch traced here: 348 us
  blocking collectives  156 us (45%)
  waiting for transfers between devices  85.1 us (24%)
  local copies, waits for them, and re-layouts  41.6 us (12%)
  matrix products  28.3 us (8%)
  other arithmetic  16.1 us (5%)
  between operations  14 us (4%)
  starting transfers between devices  6.93 us (2%)
    psum x1, blocking collectives, on_device(): bias_grad = lax.psum(jnp.sum(own_grad.astype(F32), axis=0), ('grp', 'tp'))  139 us
    psum x1, waiting for transfers between devices, on_device(): total = lax.psum((text_part + image_part).astype(BF16), 'grp').astype(F32)  50.3 us
    reduce_scatter x1, waiting for transfers between devices, on_device(): projected = lax.psum_scatter(partial, 'tp', scatter_dimension=0, tiled=True)  34.7 us
    psum x1, blocking collectives, on_device(): lax.psum(jnp.concatenate([jnp.sum(text32 * text32, axis=1), image_squares...  17.7 us
    unnamed x47, local copies, waits for them, and re-layouts  16 us
    gather x2, local copies, waits for them, and re-layouts, on_device(): placed = jnp.take(image_keys, source.reshape(rows), axis=0, mode='clip')  10 us
    dot_general x1, matrix products, on_device(): jnp.dot(text_embeds, scaled_weight, preferred_element_type=F32)  9.57 us
    dot_general x1, matrix products, on_device(): lax.dot_general(text_embeds, text_grad, over_rows, preferred_element_type...  9.33 us
  transfers between devices with their start and end apart: 4, of which 2 were waited for; matrix products, arithmetic and copies ran while one was open for 12% of the time, Pallas kernels for 0%

commit v1 on v0

--- a/solution.py
+++ b/solution.py
@@ -6,6 +6,7 @@
 EPS = 1e-06
 F32 = jnp.float32
 BF16 = jnp.bfloat16
+fill_things = lambda vals: jnp.sum(jax.lax.all_gather(vals, ("grp", "tp")), axis=0)
 
 
 def on_device(
@@ -37,7 +38,7 @@
         (key_cotangent.astype(F32) * own_valid[:, None]).astype(BF16)
     )
     masked_grad = lax.all_gather(own_grad, "tp", axis=0, tiled=True)
-    bias_grad = lax.psum(jnp.sum(own_grad.astype(F32), axis=0), ("grp", "tp"))
+    bias_grad = fill_things(jnp.sum(own_grad.astype(F32), axis=0))
     text32 = text_embeds.astype(F32)
     image32 = image_embeds.astype(F32)
     image_squares = lax.dynamic_update_slice_in_dim(

time: 349 us -> 387 us (1.11)
  blocking collectives: 156 us -> 195 us
    all_gather x0 -> x1, blocking collectives: none -> 179 us  [jax.lax.all_gather(vals, ('grp', 'tp'))]
    psum x1 -> x0, blocking collectives: 139 us -> none  [on_device(): bias_grad = lax.psum(jnp.sum(own_grad.astype(F32), axis=0), ('grp', 'tp'))]
  transfers between devices with their start and end apart: 4 -> 4, of which waited for: 2 -> 2; matrix products, arithmetic and copies ran while one was open for 12% -> 11% of each run, Pallas kernels for 0% -> 0%
where the time goes in v1:
time: 387 us
  blocking collectives  195 us (50%)
  waiting for transfers between devices  84 us (22%)
  local copies, waits for them, and re-layouts  41.6 us (11%)
  matrix products  28.6 us (7%)
  other arithmetic  16.7 us (4%)
  between operations  14 us (4%)
  starting transfers between devices  6.93 us (2%)
    all_gather x1, blocking collectives, jax.lax.all_gather(vals, ('grp', 'tp'))  179 us
    psum x1, waiting for transfers between devices, on_device(): total = lax.psum((text_part + image_part).astype(BF16), 'grp').astype(F32)  49.2 us
    reduce_scatter x1, waiting for transfers between devices, on_device(): projected = lax.psum_scatter(partial, 'tp', scatter_dimension=0, tiled=True)  34.7 us
    unnamed x47, local copies, waits for them, and re-layouts  16 us
    psum x1, blocking collectives, on_device(): lax.psum(jnp.concatenate([jnp.sum(text32 * text32, axis=1), image_squares...  15.7 us
    gather x2, local copies, waits for them, and re-layouts, on_device(): placed = jnp.take(image_keys, source.reshape(rows), axis=0, mode='clip')  10 us
    dot_general x1, matrix products, on_device(): jnp.dot(text_embeds, scaled_weight, preferred_element_type=F32)  9.85 us
    dot_general x1, matrix products, on_device(): lax.dot_general(text_embeds, text_grad, over_rows, preferred_element_type...  9.33 us
  transfers between devices with their start and end apart: 4, of which 2 were waited for; matrix products, arithmetic and copies ran while one was open for 11% of the time, Pallas kernels for 0%

profile of v1, /device:TPU:0, one launch (start us, length us, event | category | flops | bytes accessed | tf_op | source)
XLA Modules:
  0.0 386.6 jit_solution(9884755786478775773)
XLA Ops:
  7.2 6.4 %copy.37 = bf16[256,8192]{0,1:T(8,128)(2,1)} copy(bf16[256,8192]{1,0:T(8,128)(2,1)} %param.10) | data formatting | bytes 8388608 | tf_op args[1]
  13.6 6.6 %all-to-all-start = ((bf16[256,4,2048]{0,2,1:T(8,128)(2,1)}), bf16[256,4,2048]{0,2,1:T(8,128)(2,1)}, u32[]{:S(2)}, u32[]{:S(2)}) async-start(bf16[256,4,2048]{0,2,1:T(8,128)(2,1)} %bitcast.75), calls=%async_computation | async-start | bytes 8388608 | tf_op jit(solution)/shard_map/all_to_all | solution.py:33
  20.3 0.2 copy.41
  20.6 0.9 multiply_convert_fusion.7
  21.6 0.2 slice_reduce_fusion.1
  21.8 0.2 add_reduce_fusion.1
  22.0 0.1 and_or_fusion
  22.8 2.5 copy.36
  25.6 0.2 convert_reduce_fusion
  25.7 179.0 %all-gather.1 = f32[32,1,512]{2,1,0:T(1,128)S(1)} all-gather(f32[1,1,512]{2,1,0:T(1,128)S(1)} %bitcast.89), channel_id=2, replica_groups=mesh['grp'=8,'tp'=4] {'grp','tp'}, dimensions={0}, use_global_device_ids=true | all-gather | bytes 67584 | tf_op jit(solution)/shard_map/all_gather | solution.py:9
  204.7 0.6 reduce_sum.48
  205.4 3.1 multiply_reduce_fusion.1
  208.5 0.3 dynamic_update_slice.3
  208.8 5.1 %multiply_reduce_fusion = f32[2048]{0:T(1024)S(1)} fusion(bf16[2048,2048]{1,0:T(8,128)(2,1)} %param.9), kind=kLoop, calls=%fused_computation.2 | loop fusion | flops 12580864 | bytes 8396800 | tf_op jit(solution)/shard_map/reduce_sum | solution.py:47
  213.8 15.7 %psum.14 = f32[3072]{0:T(1024)S(1)} all-reduce(f32[3072]{0:T(1024)S(1)} %pad_maximum_fusion), channel_id=1, replica_groups=mesh['grp'=8,'tp'=4] {'tp'}, use_global_device_ids=true, to_apply=%region_2.0 | all-reduce | flops 3072 | bytes 24576 | tf_op jit(solution)/shard_map/psum | solution.py:47
  229.7 2.9 copy.42
  232.6 5.1 %gather_fusion.1 = bf16[1024,512]{1,0:T(8,128)(2,1)} fusion(bf16[2048,512]{1,0:T(8,128)(2,1)S(1)} %copy.42, s32[1024]{0:T(1024)S(1)} %broadcast_clamp_fusion.1), kind=kCustom, calls=%fused_computation.1 | custom fusion | bytes 2101248 | tf_op jit(solution)/shard_map/jit(_take)/gather | solution.py:73
  237.6 6.3 %copy.38 = bf16[4,256,2048]{2,1,0:T(8,128)(2,1)} copy(bf16[4,256,2048]{1,2,0:T(8,128)(2,1)} %bitcast.1) | data formatting | bytes 8388608 | tf_op jit(solution)/shard_map/all_to_all | solution.py:33
  244.0 4.6 %fusion.11 = bf16[1024,512]{0,1:T(8,128)(2,1)S(1)} fusion(bf16[1024,2048]{1,0:T(8,128)(2,1)} %bitcast.73, bf16[2048,512]{0,1:T(8,128)(2,1)S(1)} %copy-done, f32[2048]{0:T(1024)S(1)} %convert_element_type.85, f32[1024]{0:T(1024)S(1)} %get-tuple-element.33), kind=kOutput, calls=%fused_computation.19 | convolution fusion | flops 2151677952 | bytes 7352320 | tf_op jit(solution)/shard_map/dot_general | solution.py:78
  248.6 0.5 copy.39
  249.1 7.5 %gather_fusion = bf16[2048,512]{1,0:T(8,128)(2,1)S(1)} fusion(bf16[1024,512]{1,0:T(8,128)(2,1)S(1)} %copy.39, s32[2048]{0:T(1024)S(1)} %broadcast_clamp_fusion), kind=kCustom, calls=%fused_computation | custom fusion | bytes 4202496 | tf_op jit(solution)/shard_map/jit(_take)/gather | solution.py:80
  256.7 2.5 copy.40
  259.2 4.9 %fusion.14 = f32[512,2048]{1,0:T(8,128)S(1)} fusion(bf16[1024,2048]{1,0:T(8,128)(2,1)} %bitcast.74, bf16[1024,512]{1,0:T(8,128)(2,1)S(1)} %copy-done.2, f32[1024]{0:T(1024)S(1)} %get-tuple-element.32), kind=kOutput, calls=%fused_computation.20 | convolution fusion | flops 2149056512 | bytes 9441280 | tf_op jit(solution)/shard_map/dot_general | solution.py:87
  264.1 9.3 %fusion.3 = bf16[2048,512]{0,1:T(8,128)(2,1)} fusion(f32[512,2048]{1,0:T(8,128)S(1)} %fusion.14, bf16[2048,2048]{1,0:T(8,128)(2,1)} %param.9, bf16[2048,512]{0,1:T(8,128)(2,1)S(1)} %copy-done.5, f32[2048]{0:T(1024)S(1)} %slice_multiply_fusion), kind=kOutput, calls=%fused_computation.13 | convolution fusion | flops 4300210176 | bytes 16785408 | tf_op jit(solution)/shard_map/dot_general | solution.py:76
  273.4 0.3 reduce-scatter.2.cloned.1.call-start
  273.7 9.9 %fusion.4 = bf16[2048,512]{0,1:T(8,128)(2,1)} fusion(bf16[2048,512]{0,1:T(8,128)(2,1)} %copy.40, bf16[2048,2048]{1,0:T(8,128)(2,1)} %param.9, f32[2048]{0:T(1024)S(1)} %slice_multiply_fusion, pred[2048]{0:T(1024)(128)(4,1)S(1)} %or.12, bf16[2048,512]{0,1:T(8,128)(2,1)S(1)} %copy-done.1, f32[2048]{0:T(1024)S(1)} %convert_element_type.85), kind=kOutput, calls=%fused_computation.14 | convolution fusion | flops 4301258752 | bytes 14698496 | tf_op jit(solution)/shard_map/dot_general | solution.py:64
  283.6 49.2 %all-reduce.2.cloned.1.call-done = bf16[2048,512]{0,1:T(8,128)(2,1)} async-done(((bf16[2048,512]{0,1:T(8,128)(2,1)}), bf16[2048,512]{0,1:T(8,128)(2,1)}) %all-reduce.2.cloned.1.call-update) | async-done | bytes 2097168 | tf_op jit(solution)/shard_map/psum | solution.py:88
  332.8 4.9 %fusion.1 = (f32[2048]{0:T(1024)}, f32[2048,512]{0,1:T(8,128)}) fusion(bf16[2048,512]{0,1:T(8,128)(2,1)S(1)} %copy-done.1, bf16[2048,512]{0,1:T(8,128)(2,1)} %all-reduce.2.cloned.1.call-done, f32[2048]{0:T(1024)S(1)} %convert_element_type.85), kind=kLoop, calls=%fused_computation.8 | loop fusion | flops 5240832 | bytes 8404992 | tf_op jit(solution)/shard_map/reduce_sum | solution.py:90
  337.7 5.4 %copy.44 = f32[2048,512]{1,0:T(8,128)} copy(f32[2048,512]{0,1:T(8,128)} %get-tuple-element.31) | data formatting | bytes 8388608
  343.1 34.7 %reduce-scatter.2.cloned.1.call-done = bf16[512,512]{0,1:T(8,128)(2,1)} async-done(((bf16[2048,512]{0,1:T(8,128)(2,1)}), bf16[512,512]{0,1:T(8,128)(2,1)}) %reduce-scatter.2.cloned.1.call-update) | async-done | bytes 524304 | tf_op jit(solution)/shard_map/reduce_scatter | solution.py:83
  377.8 1.2 multiply_convert_fusion.6
  379.1 1.0 copy.43
  (70 shorter events, 1.3 us)
Async XLA Ops:
  13.5 6.7 %copy-start.10 = (s32[2]{0:T(128)S(1)}, s32[2]{0:T(128)}, u32[]{:S(2)}) copy-start(s32[2]{0:T(128)} %param.13) | copy-start | bytes 28
  13.5 6.7 %copy-start.6 = (bf16[512,512]{1,0:T(8,128)(2,1)S(1)}, bf16[512,512]{1,0:T(8,128)(2,1)}, u32[]{:S(2)}) copy-start(bf16[512,512]{1,0:T(8,128)(2,1)} %param.17) | copy-start | bytes 1572868
  13.5 8.0 %copy-start.11 = (s32[2]{0:T(128)S(1)}, s32[2]{0:T(128)}, u32[]{:S(2)}) copy-start(s32[2]{0:T(128)} %param.12) | copy-start | bytes 28
  13.5 8.3 %copy-start.7 = (s32[2,2]{1,0:T(2,128)S(1)}, s32[2,2]{1,0:T(2,128)}, u32[]{:S(2)}) copy-start(s32[2,2]{1,0:T(2,128)} %param.11) | copy-start | bytes 52
  13.5 9.3 %copy-start.4 = (bf16[2048,512]{1,0:T(8,128)(2,1)S(1)}, bf16[2048,512]{1,0:T(8,128)(2,1)}, u32[]{:S(2)}) copy-start(bf16[2048,512]{1,0:T(8,128)(2,1)} %param.15) | copy-start | bytes 6291460
  13.6 224.1 %all-to-all-start = ((bf16[256,4,2048]{0,2,1:T(8,128)(2,1)}), bf16[256,4,2048]{0,2,1:T(8,128)(2,1)}, u32[]{:S(2)}, u32[]{:S(2)}) async-start(bf16[256,4,2048]{0,2,1:T(8,128)(2,1)} %bitcast.75), calls=%async_computation | async-start | bytes 8388608 | tf_op jit(solution)/shard_map/all_to_all | solution.py:33
  20.2 5.2 %copy-start.8 = (bf16[2048]{0:T(1024)(128)(2,1)S(1)}, bf16[2048]{0:T(1024)(128)(2,1)}, u32[]{:S(2)}) copy-start(bf16[2048]{0:T(1024)(128)(2,1)} %param.14) | copy-start | bytes 12292
  20.2 209.5 %all-gather.4.cloned.1.call-start = ((), (), s32[]{:S(2)}) async-start(), calls=%async_computation.2 | async-start | bytes 2621440 | tf_op jit(solution)/shard_map/all_gather | solution.py:40
  21.5 4.1 %copy-start.3 = (bf16[512,512]{0,1:T(8,128)(2,1)S(1)}, bf16[512,512]{0,1:T(8,128)(2,1)}, u32[]{:S(2)}) copy-start(bf16[512,512]{0,1:T(8,128)(2,1)} %multiply_convert_fusion.7) | copy-start | bytes 1572868
  21.5 311.3 %all-reduce.2.cloned.1.call-start = ((), (), s32[]{:S(2)}) async-start(), calls=%async_computation.4 | async-start | bytes 4194304 | tf_op jit(solution)/shard_map/psum | solution.py:88
  237.6 6.4 %copy-start = (bf16[2048,512]{0,1:T(8,128)(2,1)S(1)}, bf16[2048,512]{0,1:T(8,128)(2,1)}, u32[]{:S(2)}) copy-start(bf16[2048,512]{0,1:T(8,128)(2,1)} %copy.36) | copy-start | bytes 6291460
  256.7 2.5 copy-start.2
  259.2 4.9 %copy-start.5 = (bf16[2048,512]{0,1:T(8,128)(2,1)S(1)}, bf16[2048,512]{0,1:T(8,128)(2,1)}, u32[]{:S(2)}) copy-start(bf16[2048,512]{0,1:T(8,128)(2,1)} %all-gather.4.cloned.1.call-done) | copy-start | bytes 6291460
  264.1 9.6 %copy-start.1 = (bf16[2048,512]{0,1:T(8,128)(2,1)S(1)}, bf16[2048,512]{0,1:T(8,128)(2,1)}, u32[]{:S(2)}) copy-start(bf16[2048,512]{0,1:T(8,128)(2,1)} %copy.36) | copy-start | bytes 6291460
  273.4 10.2 %copy-start.9 = (bf16[512]{0:T(512)(128)(2,1)S(1)}, bf16[512]{0:T(512)(128)(2,1)}, u32[]{:S(2)}) copy-start(bf16[512]{0:T(512)(128)(2,1)} %param.16) | copy-start | bytes 3076
  273.4 104.4 %reduce-scatter.2.cloned.1.call-start = ((), (), s32[]{:S(2)}) async-start(), calls=%async_computation.3 | async-start | bytes 2621440 | tf_op jit(solution)/shard_map/reduce_scatter | solution.py:83
Sparse Core Ops, SparseCore 0:
  23.1 77.2 all-gather.3
  273.6 59.1 all-reduce.1
  335.1 42.6 reduce-scatter.1
